TPU v7x, 32 devices: a whole 2x2x4 slice. The times are simulated.
32 devices in a mesh: groups: 2 (over y), head: 8 (over z, x), blk: 2 (over core).
Axes of the slice: x: 2, y: 2, z: 4, core: 2. Of those that a mesh axis runs over, the one named last changes fastest.
Arguments:
- queries: bfloat16 [1024, 2048], P(('groups', 'head', 'blk')), parts along dimension 0, may hold values from -6 to 6
- key_rows: bfloat16 [1024, 256], P(('groups', 'head', 'blk')), parts along dimension 0, may hold values from -6 to 6
- value_rows: bfloat16 [1024, 256], P(('groups', 'head', 'blk')), parts along dimension 0, may hold values from -6 to 6
- fwd_output: bfloat16 [1024, 2048], P(('groups', 'head', 'blk')), parts along dimension 0, may hold values from -6 to 6
- grad_out: bfloat16 [1024, 2048], P(('groups', 'head', 'blk')), parts along dimension 0, may hold values from -6 to 6
- log_norm: float32 [1024, 16], P(('groups', 'head', 'blk')), parts along dimension 0, may hold values from 2 to 5.5
- visible: int32 [8, 4], P('groups'), parts along dimension 0, may hold values from 0 to 1, as said below
- seg_lengths: int32 [8], P('groups'), parts along dimension 0, may hold values from 1 to 256, 512 in all
Outputs:
- grad_queries: bfloat16 [1024, 2048], P(('groups', 'head', 'blk')), parts along dimension 0
- grad_keys: bfloat16 [1024, 256], P(('groups', 'head', 'blk')), parts along dimension 0
- grad_values: bfloat16 [1024, 256], P(('groups', 'head', 'blk')), parts along dimension 0
There are 2 independent parts, one for each index of `groups`. A program takes and returns all parts, laid end to end along the dimension named above; each array names one. Nothing has to cross between parts.
Inputs may be any that keep to these rules, and one draw needn't show every extreme that they name: visible[a, b] is 1 exactly when block b is block a or an ancestor of block a in a tree over the 4 blocks whose root is block 0 and in which every block's parent comes before it.
All inputs are finite; a program needn't handle non-finite values.
Results may differ from a plain program's by a relative error of at most 0.0051.
Values may be sent and summed in bfloat16 or wider, within the bound.
A program may use at most 64 MiB of HBM per device.

v0:
```python
import math
import jax
import jax.numpy as jnp
from jax import lax
from jax.sharding import PartitionSpec as P

BLOCK = 128
top_precision = lax.Precision.HIGHEST


def from_behind(value, axis, steps):
    count = lax.axis_size(axis)
    pairs = [(source, (source + steps) % count) for source in range(count)]
    return lax.ppermute(value, axis, pairs)


def token_spots(row_count, tok_rows, cycle_size, cycle_owner):
    iota_rows = jnp.arange(row_count, dtype=jnp.int32)
    return (
        iota_rows // tok_rows * (cycle_size * tok_rows)
        + cycle_owner * tok_rows
        + iota_rows % tok_rows
    )


def allowed_pairs(query_pos, key_pos, visible_f, seg_ends):
    block_iota = jnp.arange(visible_f.shape[0], dtype=jnp.int32)
    query_block = query_pos // BLOCK
    key_block = key_pos // BLOCK
    query_hot = (query_block[:, None] == block_iota[None, :]).astype(jnp.float32)
    key_hot = (key_block[:, None] == block_iota[None, :]).astype(jnp.float32)
    reach_rows = jnp.dot(query_hot, visible_f, precision=top_precision)
    reach_table = jnp.dot(reach_rows, key_hot.T, precision=top_precision)
    query_doc = jnp.sum((query_pos[:, None] >= seg_ends[None, :]).astype(jnp.int32), axis=1)
    key_doc = jnp.sum((key_pos[:, None] >= seg_ends[None, :]).astype(jnp.int32), axis=1)
    earlier = (query_block[:, None] != key_block[None, :]) | (
        key_pos[None, :] <= query_pos[:, None]
    )
    return (reach_table > 0.5) & (query_doc[:, None] == key_doc[None, :]) & earlier


def tile_grads(query_part, grad_rows, lse_rows, delta_rows, key_part, value_part, allowed):
    softmax_scale = 1.0 / math.sqrt(query_part.shape[2])
    scores = (
        jnp.einsum("qhd,khd->hqk", query_part, key_part, preferred_element_type=jnp.float32)
        * softmax_scale
    )
    prob_full = jnp.where(allowed[None], jnp.exp(scores - lse_rows.T[:, :, None]), 0.0)
    prob_half = prob_full.astype(jnp.bfloat16)
    value_grad = jnp.einsum(
        "hqk,qhd->khd", prob_half, grad_rows, preferred_element_type=jnp.float32
    )
    grad_prob = jnp.einsum(
        "qhd,khd->hqk", grad_rows, value_part, preferred_element_type=jnp.float32
    )
    grad_score = (prob_full * (grad_prob - delta_rows.T[:, :, None]) * softmax_scale).astype(
        jnp.bfloat16
    )
    query_grad = jnp.einsum(
        "hqk,khd->qhd", grad_score, key_part, preferred_element_type=jnp.float32
    )
    key_grad = jnp.einsum(
        "hqk,qhd->khd", grad_score, query_part, preferred_element_type=jnp.float32
    )
    return (query_grad, key_grad, value_grad)


def shards(queries, key_rows, value_rows, fwd_output, grad_out, log_norm, visible, seg_lengths):
    tok_rows, model_width = queries.shape
    head_total = log_norm.shape[1]
    head_dim = model_width // head_total
    kv_total = key_rows.shape[1] // head_dim
    group_size = head_total // kv_total
    query_heads = queries.reshape(tok_rows, head_total, head_dim)
    grad_heads = grad_out.reshape(tok_rows, head_total, head_dim)
    out_heads = fwd_output.reshape(tok_rows, head_total, head_dim)
    row_delta = jnp.sum(grad_heads.astype(jnp.float32) * out_heads.astype(jnp.float32), axis=2)
    key_heads = jnp.repeat(key_rows.reshape(tok_rows, kv_total, head_dim), group_size, axis=1)
    value_heads = jnp.repeat(value_rows.reshape(tok_rows, kv_total, head_dim), group_size, axis=1)
    local_q, local_g, local_k, local_v = (
        lax.all_to_all(query_heads, "head", split_axis=1, concat_axis=0, tiled=True),
        lax.all_to_all(grad_heads, "head", split_axis=1, concat_axis=0, tiled=True),
        lax.all_to_all(key_heads, "head", split_axis=1, concat_axis=0, tiled=True),
        lax.all_to_all(value_heads, "head", split_axis=1, concat_axis=0, tiled=True),
    )
    local_lse, local_delta = (
        lax.all_to_all(log_norm, "head", split_axis=1, concat_axis=0, tiled=True),
        lax.all_to_all(row_delta, "head", split_axis=1, concat_axis=0, tiled=True),
    )
    row_count = local_q.shape[0]
    cycle_size = lax.axis_size("blk")
    cycle_owner = lax.axis_index("blk")
    query_pos = token_spots(row_count, tok_rows, cycle_size, cycle_owner)
    visible_f = visible.astype(jnp.float32)
    seg_ends = jnp.cumsum(seg_lengths)

    def pair_grads(key_part, value_part, source):
        key_pos = token_spots(row_count, tok_rows, cycle_size, source)
        allowed = allowed_pairs(query_pos, key_pos, visible_f, seg_ends)
        return tile_grads(local_q, local_g, local_lse, local_delta, key_part, value_part, allowed)

    zero_grads = jnp.zeros(local_k.shape, jnp.float32)

    def one_turn(turn_index, carry_state):
        key_now, value_now, key_acc, value_acc, query_acc = carry_state
        source = (cycle_owner - turn_index) % cycle_size
        query_part, key_part, value_part = pair_grads(key_now, value_now, source)
        key_now, value_now = from_behind((key_now, value_now), "blk", 1)
        key_acc, value_acc = from_behind((key_acc + key_part, value_acc + value_part), "blk", 1)
        return (key_now, value_now, key_acc, value_acc, query_acc + query_part)

    start_state = (local_k, local_v, zero_grads, zero_grads, zero_grads)
    final_state = lax.fori_loop(0, cycle_size, one_turn, start_state)
    key_grad, value_grad, query_grad = (final_state[2], final_state[3], final_state[4])
    query_home = lax.all_to_all(
        query_grad.astype(jnp.bfloat16), "head", split_axis=0, concat_axis=1, tiled=True
    )
    grad_queries = query_home.reshape(tok_rows, model_width)
    key_home, value_home = (
        lax.all_to_all(key_grad, "head", split_axis=0, concat_axis=1, tiled=True),
        lax.all_to_all(value_grad, "head", split_axis=0, concat_axis=1, tiled=True),
    )
    key_total = jnp.sum(key_home.reshape(tok_rows, kv_total, group_size, head_dim), axis=2)
    value_total = jnp.sum(value_home.reshape(tok_rows, kv_total, group_size, head_dim), axis=2)
    grad_keys = key_total.reshape(tok_rows, kv_total * head_dim).astype(jnp.bfloat16)
    grad_values = value_total.reshape(tok_rows, kv_total * head_dim).astype(jnp.bfloat16)
    return (grad_queries, grad_keys, grad_values)


def solution(mesh):
    return jax.shard_map(
        shards,
        mesh=mesh,
        in_specs=(
            P(("groups", "head", "blk"), None),
            P(("groups", "head", "blk"), None),
            P(("groups", "head", "blk"), None),
            P(("groups", "head", "blk"), None),
            P(("groups", "head", "blk"), None),
            P(("groups", "head", "blk"), None),
            P("groups", None),
            P("groups"),
        ),
        out_specs=(
            P(("groups", "head", "blk"), None),
            P(("groups", "head", "blk"), None),
            P(("groups", "head", "blk"), None),
        ),
        check_vma=False,
    )
```

profile of v0, /device:TPU:0, one launch (start us, length us, event | category | flops | bytes accessed | tf_op | source)
XLA Modules:
  0.0 115.2 jit_solution(6683661105864896199)
XLA Ops:
  0.6 1.0 convert_bitcast_fusion
  1.7 0.8 copy-done.1
  2.8 13.7 %all_to_all.143 = f32[32,8,2]{0,2,1:T(2,128)S(1)} all-to-all(f32[32,8,2]{0,2,1:T(2,128)S(1)} %bitcast.160), channel_id=1, replica_groups=mesh['groups'=2,'head'=8,'blk'=2] {'head'}, dimensions={1} | all-to-all | bytes 4096 | tf_op jit(solution)/shard_map/all_to_all | solution.py:88
  16.4 3.3 %all-to-all-start.3 = ((f32[32,8,2]{0,2,1:T(2,128)}), f32[32,8,2]{0,2,1:T(2,128)S(1)}, u32[]{:S(2)}, u32[]{:S(2)}) async-start(f32[32,8,2]{0,2,1:T(2,128)} %bitcast.13), calls=%async_computation.3 | async-start | bytes 16384 | tf_op jit(solution)/shard_map/all_to_all | solution.py:87
  19.8 6.4 %all-to-all-done.3 = f32[32,8,2]{0,2,1:T(2,128)S(1)} async-done(((f32[32,8,2]{0,2,1:T(2,128)}), f32[32,8,2]{0,2,1:T(2,128)S(1)}, u32[]{:S(2)}, u32[]{:S(2)}) %all-to-all-start.3) | async-done | bytes 2080 | tf_op jit(solution)/shard_map/all_to_all | solution.py:87
  26.9 3.5 %all-to-all-start = ((bf16[32,16,128]{2,0,1:T(8,128)(2,1)}), bf16[32,16,128]{2,0,1:T(8,128)(2,1)S(1)}, u32[]{:S(2)}, u32[]{:S(2)}) async-start(bf16[32,16,128]{2,0,1:T(8,128)(2,1)} %bitcast), calls=%async_computation | async-start | bytes 262144 | tf_op jit(solution)/shard_map/all_to_all | solution.py:83
  30.5 7.3 %all-to-all-done = bf16[32,16,128]{2,0,1:T(8,128)(2,1)S(1)} async-done(((bf16[32,16,128]{2,0,1:T(8,128)(2,1)}), bf16[32,16,128]{2,0,1:T(8,128)(2,1)S(1)}, u32[]{:S(2)}, u32[]{:S(2)}) %all-to-all-start) | async-done | bytes 131104 | tf_op jit(solution)/shard_map/all_to_all | solution.py:83
  38.4 3.4 %all-to-all-start.1 = ((bf16[32,16,128]{2,0,1:T(8,128)(2,1)}), bf16[32,16,128]{2,0,1:T(8,128)(2,1)S(1)}, u32[]{:S(2)}, u32[]{:S(2)}) async-start(bf16[32,16,128]{2,0,1:T(8,128)(2,1)} %bitcast.4), calls=%async_computation.1 | async-start | bytes 262144 | tf_op jit(solution)/shard_map/all_to_all | solution.py:84
  42.5 6.6 %all-to-all-done.1 = bf16[32,16,128]{2,0,1:T(8,128)(2,1)S(1)} async-done(((bf16[32,16,128]{2,0,1:T(8,128)(2,1)}), bf16[32,16,128]{2,0,1:T(8,128)(2,1)S(1)}, u32[]{:S(2)}, u32[]{:S(2)}) %all-to-all-start.1) | async-done | bytes 131104 | tf_op jit(solution)/shard_map/all_to_all | solution.py:84
  49.0 3.4 %all-to-all-start.2 = ((bf16[32,16,128]{2,0,1:T(8,128)(2,1)}), bf16[32,16,128]{2,0,1:T(8,128)(2,1)S(1)}, u32[]{:S(2)}, u32[]{:S(2)}) async-start(bf16[32,16,128]{2,0,1:T(8,128)(2,1)} %copy_bitcast_fusion.1), calls=%async_computation.2 | async-start | bytes 262144 | tf_op jit(solution)/shard_map/all_to_all | solution.py:81
  53.1 6.6 %all-to-all-done.2 = bf16[32,16,128]{2,0,1:T(8,128)(2,1)S(1)} async-done(((bf16[32,16,128]{2,0,1:T(8,128)(2,1)}), bf16[32,16,128]{2,0,1:T(8,128)(2,1)S(1)}, u32[]{:S(2)}, u32[]{:S(2)}) %all-to-all-start.2) | async-done | bytes 131104 | tf_op jit(solution)/shard_map/all_to_all | solution.py:81
  59.7 3.5 %all-to-all-start.4 = ((bf16[32,16,128]{2,0,1:T(8,128)(2,1)}), bf16[32,16,128]{2,0,1:T(8,128)(2,1)S(1)}, u32[]{:S(2)}, u32[]{:S(2)}) async-start(bf16[32,16,128]{2,0,1:T(8,128)(2,1)} %copy_bitcast_fusion), calls=%async_computation.4 | async-start | bytes 262144 | tf_op jit(solution)/shard_map/all_to_all | solution.py:82
  64.4 6.1 %all-to-all-done.4 = bf16[32,16,128]{2,0,1:T(8,128)(2,1)S(1)} async-done(((bf16[32,16,128]{2,0,1:T(8,128)(2,1)}), bf16[32,16,128]{2,0,1:T(8,128)(2,1)S(1)}, u32[]{:S(2)}, u32[]{:S(2)}) %all-to-all-start.4) | async-done | bytes 131104 | tf_op jit(solution)/shard_map/all_to_all | solution.py:82
  70.6 8.2 %while.29 = (s32[]{:T(128)}, bf16[256,2,128]{2,0,1:T(8,128)(2,1)S(1)}, bf16[256,2,128]{2,0,1:T(8,128)(2,1)S(1)}, f32[256,2,128]{2,0,1:T(8,128)S(1)}, f32[256,2,1...) while((s32[]{:T(128)}, ...), condition=%wide.region_5.6_spmd.clone.clone.clone, body=%wide.region_2.5_spmd.clone.clone.clone.sunk | while | flops 172717072 | bytes 8807412 | solution.py:113
  77.8 0.8 collective-permute-done
  78.8 0.9 copy.127
  79.7 3.4 %all-to-all-start.6 = ((bf16[256,2,128]{2,1,0:T(2,128)(2,1)}), bf16[256,2,128]{2,1,0:T(2,128)(2,1)S(1)}, u32[]{:S(2)}, u32[]{:S(2)}) async-start(bf16[256,2,128]{2,1,0:T(2,128)(2,1)} %copy.127), calls=%async_computation.6 | async-start | bytes 262144 | tf_op jit(solution)/shard_map/all_to_all | solution.py:115
  83.1 0.9 copy.106
  83.9 6.6 %all-to-all-done.6 = bf16[256,2,128]{2,1,0:T(2,128)(2,1)S(1)} async-done(((bf16[256,2,128]{2,1,0:T(2,128)(2,1)}), bf16[256,2,128]{2,1,0:T(2,128)(2,1)S(1)}, u32[]{:S(2)}, u32[]{:S(2)}) %all-to-all-start.6) | async-done | bytes 131104 | tf_op jit(solution)/shard_map/all_to_all | solution.py:115
  90.6 3.4 %all-to-all-start.7 = ((f32[256,2,128]{2,1,0:T(2,128)}), f32[256,2,128]{2,1,0:T(2,128)S(1)}, u32[]{:S(2)}, u32[]{:S(2)}) async-start(f32[256,2,128]{2,1,0:T(2,128)} %copy.106), calls=%async_computation.7 | async-start | bytes 524288 | tf_op jit(solution)/shard_map/all_to_all | solution.py:120
  94.0 0.9 copy.108
  94.9 7.4 %all-to-all-done.7 = f32[256,2,128]{2,1,0:T(2,128)S(1)} async-done(((f32[256,2,128]{2,1,0:T(2,128)}), f32[256,2,128]{2,1,0:T(2,128)S(1)}, u32[]{:S(2)}, u32[]{:S(2)}) %all-to-all-start.7) | async-done | bytes 262176 | tf_op jit(solution)/shard_map/all_to_all | solution.py:120
  102.3 3.4 %all-to-all-start.8 = ((f32[256,2,128]{2,1,0:T(2,128)}), f32[256,2,128]{2,1,0:T(2,128)S(1)}, u32[]{:S(2)}, u32[]{:S(2)}) async-start(f32[256,2,128]{2,1,0:T(2,128)} %copy.108), calls=%async_computation.8 | async-start | bytes 524288 | tf_op jit(solution)/shard_map/all_to_all | solution.py:121
  106.8 7.4 %all-to-all-done.8 = f32[256,2,128]{2,1,0:T(2,128)S(1)} async-done(((f32[256,2,128]{2,1,0:T(2,128)}), f32[256,2,128]{2,1,0:T(2,128)S(1)}, u32[]{:S(2)}, u32[]{:S(2)}) %all-to-all-start.8) | async-done | bytes 262176 | tf_op jit(solution)/shard_map/all_to_all | solution.py:121
  (85 shorter events, 13.5 us)
Async XLA Ops:
  0.6 41.1 %copy-start = (bf16[32,2048]{1,0:T(8,128)(2,1)S(1)}, bf16[32,2048]{1,0:T(8,128)(2,1)}, u32[]{:S(2)}) copy-start(bf16[32,2048]{1,0:T(8,128)(2,1)} %param.10) | copy-start | bytes 393220
  1.6 0.9 copy-start.1
  2.8 17.0 %copy-start.2 = (bf16[32,256]{1,0:T(8,128)(2,1)S(1)}, bf16[32,256]{1,0:T(8,128)(2,1)}, u32[]{:S(2)}) copy-start(bf16[32,256]{1,0:T(8,128)(2,1)} %param.11) | copy-start | bytes 49156
  16.4 9.8 %all-to-all-start.3 = ((f32[32,8,2]{0,2,1:T(2,128)}), f32[32,8,2]{0,2,1:T(2,128)S(1)}, u32[]{:S(2)}, u32[]{:S(2)}) async-start(f32[32,8,2]{0,2,1:T(2,128)} %bitcast.13), calls=%async_computation.3 | async-start | bytes 16384 | tf_op jit(solution)/shard_map/all_to_all | solution.py:87
  26.9 3.5 %copy-start.3 = (bf16[32,256]{1,0:T(8,128)(2,1)S(1)}, bf16[32,256]{1,0:T(8,128)(2,1)}, u32[]{:S(2)}) copy-start(bf16[32,256]{1,0:T(8,128)(2,1)} %param.12) | copy-start | bytes 49156
  26.9 10.8 %all-to-all-start = ((bf16[32,16,128]{2,0,1:T(8,128)(2,1)}), bf16[32,16,128]{2,0,1:T(8,128)(2,1)S(1)}, u32[]{:S(2)}, u32[]{:S(2)}) async-start(bf16[32,16,128]{2,0,1:T(8,128)(2,1)} %bitcast), calls=%async_computation | async-start | bytes 262144 | tf_op jit(solution)/shard_map/all_to_all | solution.py:83
  38.4 10.7 %all-to-all-start.1 = ((bf16[32,16,128]{2,0,1:T(8,128)(2,1)}), bf16[32,16,128]{2,0,1:T(8,128)(2,1)S(1)}, u32[]{:S(2)}, u32[]{:S(2)}) async-start(bf16[32,16,128]{2,0,1:T(8,128)(2,1)} %bitcast.4), calls=%async_computation.1 | async-start | bytes 262144 | tf_op jit(solution)/shard_map/all_to_all | solution.py:84
  49.0 10.7 %all-to-all-start.2 = ((bf16[32,16,128]{2,0,1:T(8,128)(2,1)}), bf16[32,16,128]{2,0,1:T(8,128)(2,1)S(1)}, u32[]{:S(2)}, u32[]{:S(2)}) async-start(bf16[32,16,128]{2,0,1:T(8,128)(2,1)} %copy_bitcast_fusion.1), calls=%async_computation.2 | async-start | bytes 262144 | tf_op jit(solution)/shard_map/all_to_all | solution.py:81
  59.7 3.6 %copy-start.5 = (s32[4]{0:T(128)S(1)}, s32[4]{0:T(128)}, u32[]{:S(2)}) copy-start(s32[4]{0:T(128)} %param.17) | copy-start | bytes 52
  59.7 10.8 %all-to-all-start.4 = ((bf16[32,16,128]{2,0,1:T(8,128)(2,1)}), bf16[32,16,128]{2,0,1:T(8,128)(2,1)S(1)}, u32[]{:S(2)}, u32[]{:S(2)}) async-start(bf16[32,16,128]{2,0,1:T(8,128)(2,1)} %copy_bitcast_fusion), calls=%async_computation.4 | async-start | bytes 262144 | tf_op jit(solution)/shard_map/all_to_all | solution.py:82
  63.2 0.7 copy-start.4
  72.1 2.5 %collective-permute-start.2 = (f32[256,2,128]{2,0,1:T(8,128)S(1)}, f32[256,2,128]{2,0,1:T(8,128)S(1)}, u32[]{:S(2)}, u32[]{:S(2)}) collective-permute-start(f32[256,2,128]{2,0,1:T(8,128)S(1)} %fusion.84), channel_id=1, source_target_pairs={{0,1},{1,0},{2,3},{3,2},{4,5},{5,4},{6,7},{7,6},{8,9},{9,8},{10,11... | collective-permute-start | bytes 786440 | tf_op jit(solution)/shard_map/while/body/eval_jaxpr/ppermute | solution.py:14
  72.5 2.1 %collective-permute-start.3 = (f32[256,2,128]{2,0,1:T(8,128)S(1)}, f32[256,2,128]{2,0,1:T(8,128)S(1)}, u32[]{:S(2)}, u32[]{:S(2)}) collective-permute-start(f32[256,2,128]{2,0,1:T(8,128)S(1)} %fusion.85), channel_id=1, source_target_pairs={{0,1},{1,0},{2,3},{3,2},{4,5},{5,4},{6,7},{7,6},{8,9},{9,8},{10,11... | collective-permute-start | bytes 786440 | tf_op jit(solution)/shard_map/while/body/eval_jaxpr/ppermute | solution.py:14
  73.0 1.3 %collective-permute-start = (bf16[256,2,128]{2,0,1:T(8,128)(2,1)S(1)}, bf16[256,2,128]{2,0,1:T(8,128)(2,1)S(1)}, u32[]{:S(2)}, u32[]{:S(2)}) collective-permute-start(bf16[256,2,128]{2,0,1:T(8,128)(2,1)S(1)} %copy.137), channel_id=1, source_target_pairs={{0,1},{1,0},{2,3},{3,2},{4,5},{5,4},{6,7},{7,6},{8,9},{9,8},{10,11... | collective-permute-start | bytes 393224 | tf_op jit(solution)/shard_map/while/body/eval_jaxpr/ppermute | solution.py:14
  73.1 1.5 %collective-permute-start.1 = (bf16[256,2,128]{2,0,1:T(8,128)(2,1)S(1)}, bf16[256,2,128]{2,0,1:T(8,128)(2,1)S(1)}, u32[]{:S(2)}, u32[]{:S(2)}) collective-permute-start(bf16[256,2,128]{2,0,1:T(8,128)(2,1)S(1)} %copy.138), channel_id=1, source_target_pairs={{0,1},{1,0},{2,3},{3,2},{4,5},{5,4},{6,7},{7,6},{8,9},{9,8},{10,11... | collective-permute-start | bytes 393224 | tf_op jit(solution)/shard_map/while/body/eval_jaxpr/ppermute | solution.py:14
  76.1 2.7 %collective-permute-start.2 = (f32[256,2,128]{2,0,1:T(8,128)S(1)}, f32[256,2,128]{2,0,1:T(8,128)S(1)}, u32[]{:S(2)}, u32[]{:S(2)}) collective-permute-start(f32[256,2,128]{2,0,1:T(8,128)S(1)} %fusion.84), channel_id=1, source_target_pairs={{0,1},{1,0},{2,3},{3,2},{4,5},{5,4},{6,7},{7,6},{8,9},{9,8},{10,11... | collective-permute-start | bytes 786440 | tf_op jit(solution)/shard_map/while/body/eval_jaxpr/ppermute | solution.py:14
  76.8 2.0 %collective-permute-start.3 = (f32[256,2,128]{2,0,1:T(8,128)S(1)}, f32[256,2,128]{2,0,1:T(8,128)S(1)}, u32[]{:S(2)}, u32[]{:S(2)}) collective-permute-start(f32[256,2,128]{2,0,1:T(8,128)S(1)} %fusion.85), channel_id=1, source_target_pairs={{0,1},{1,0},{2,3},{3,2},{4,5},{5,4},{6,7},{7,6},{8,9},{9,8},{10,11... | collective-permute-start | bytes 786440 | tf_op jit(solution)/shard_map/while/body/eval_jaxpr/ppermute | solution.py:14
  77.0 1.6 %collective-permute-start = (bf16[256,2,128]{2,0,1:T(8,128)(2,1)S(1)}, bf16[256,2,128]{2,0,1:T(8,128)(2,1)S(1)}, u32[]{:S(2)}, u32[]{:S(2)}) collective-permute-start(bf16[256,2,128]{2,0,1:T(8,128)(2,1)S(1)} %copy.137), channel_id=1, source_target_pairs={{0,1},{1,0},{2,3},{3,2},{4,5},{5,4},{6,7},{7,6},{8,9},{9,8},{10,11... | collective-permute-start | bytes 393224 | tf_op jit(solution)/shard_map/while/body/eval_jaxpr/ppermute | solution.py:14
  77.4 1.4 %collective-permute-start.1 = (bf16[256,2,128]{2,0,1:T(8,128)(2,1)S(1)}, bf16[256,2,128]{2,0,1:T(8,128)(2,1)S(1)}, u32[]{:S(2)}, u32[]{:S(2)}) collective-permute-start(bf16[256,2,128]{2,0,1:T(8,128)(2,1)S(1)} %copy.138), channel_id=1, source_target_pairs={{0,1},{1,0},{2,3},{3,2},{4,5},{5,4},{6,7},{7,6},{8,9},{9,8},{10,11... | collective-permute-start | bytes 393224 | tf_op jit(solution)/shard_map/while/body/eval_jaxpr/ppermute | solution.py:14
  79.7 10.9 %all-to-all-start.6 = ((bf16[256,2,128]{2,1,0:T(2,128)(2,1)}), bf16[256,2,128]{2,1,0:T(2,128)(2,1)S(1)}, u32[]{:S(2)}, u32[]{:S(2)}) async-start(bf16[256,2,128]{2,1,0:T(2,128)(2,1)} %copy.127), calls=%async_computation.6 | async-start | bytes 262144 | tf_op jit(solution)/shard_map/all_to_all | solution.py:115
  90.6 11.7 %all-to-all-start.7 = ((f32[256,2,128]{2,1,0:T(2,128)}), f32[256,2,128]{2,1,0:T(2,128)S(1)}, u32[]{:S(2)}, u32[]{:S(2)}) async-start(f32[256,2,128]{2,1,0:T(2,128)} %copy.106), calls=%async_computation.7 | async-start | bytes 524288 | tf_op jit(solution)/shard_map/all_to_all | solution.py:120
  102.3 11.9 %all-to-all-start.8 = ((f32[256,2,128]{2,1,0:T(2,128)}), f32[256,2,128]{2,1,0:T(2,128)S(1)}, u32[]{:S(2)}, u32[]{:S(2)}) async-start(f32[256,2,128]{2,1,0:T(2,128)} %copy.108), calls=%async_computation.8 | async-start | bytes 524288 | tf_op jit(solution)/shard_map/all_to_all | solution.py:121
where the time goes:
time: 116 us; the launch traced here: 115 us
  waiting for transfers between devices  56.1 us (48%)
  starting transfers between devices  29.6 us (26%)
  blocking collectives  13.7 us (12%)
  local copies, waits for them, and re-layouts  8.98 us (8%)
  matrix products  3.54 us (3%)
  other arithmetic  2.25 us (2%)
    all_to_all x1, blocking collectives, shards(): lax.all_to_all(row_delta, 'head', split_axis=1, concat_axis=0, tiled=True)  13.7 us
    all_to_all x1, waiting for transfers between devices, shards(): lax.all_to_all(key_grad, 'head', split_axis=0, concat_axis=1, tiled=True)  7.38 us
    all_to_all x1, waiting for transfers between devices, shards(): lax.all_to_all(value_grad, 'head', split_axis=0, concat_axis=1, tiled=True)  7.37 us
    all_to_all x1, waiting for transfers between devices, shards(): lax.all_to_all(key_heads, 'head', split_axis=1, concat_axis=0, tiled=True)  7.25 us
    all_to_all x1, waiting for transfers between devices, shards(): lax.all_to_all(query_grad.astype(jnp.bfloat16), 'head', split_axis=0, con...  6.61 us
    all_to_all x1, waiting for transfers between devices, shards(): lax.all_to_all(query_heads, 'head', split_axis=1, concat_axis=0, tiled=True)  6.6 us
    all_to_all x1, waiting for transfers between devices, shards(): lax.all_to_all(value_heads, 'head', split_axis=1, concat_axis=0, tiled=True)  6.59 us
    all_to_all x1, waiting for transfers between devices, shards(): lax.all_to_all(log_norm, 'head', split_axis=1, concat_axis=0, tiled=True)  6.43 us
  transfers between devices with their start and end apart: 16, of which 12 were waited for; matrix products, arithmetic and copies ran while one was open for 5% of the time, Pallas kernels for 0%

commit v1 on v0

--- a/solution.py
+++ b/solution.py
@@ -6,6 +6,22 @@
 
 BLOCK = 128
 top_precision = lax.Precision.HIGHEST
+
+
+def exchange_in_pairs(x, axis, split, join):
+    ways, here = (lax.axis_size(axis), lax.axis_index(axis))
+    width = x.shape[split] // ways
+    lengths = list(x.shape)
+    lengths[split] = width
+    height = lengths[join]
+    lengths[join] = height * ways
+    full = jnp.zeros(lengths, x.dtype)
+    for mask in range(ways):
+        part = lax.dynamic_slice_in_dim(x, (here ^ mask) * width, width, axis=split)
+        if mask:
+            part = lax.ppermute(part, axis, [(d, d ^ mask) for d in range(ways)])
+        full = lax.dynamic_update_slice_in_dim(full, part, (here ^ mask) * height, axis=join)
+    return full
 
 
 def from_behind(value, axis, steps):
@@ -80,7 +96,7 @@
     local_q, local_g, local_k, local_v = (
         lax.all_to_all(query_heads, "head", split_axis=1, concat_axis=0, tiled=True),
         lax.all_to_all(grad_heads, "head", split_axis=1, concat_axis=0, tiled=True),
-        lax.all_to_all(key_heads, "head", split_axis=1, concat_axis=0, tiled=True),
+        exchange_in_pairs(key_heads, "head", 1, 0),
         lax.all_to_all(value_heads, "head", split_axis=1, concat_axis=0, tiled=True),
     )
     local_lse, local_delta = (

time: 116 us -> 109 us (0.940)
  starting transfers between devices: 29.6 us -> 47.3 us
  blocking collectives: 13.7 us -> 0 us
  waiting for transfers between devices: 56.1 us -> 45.2 us
    ppermute x0 -> x7, starting transfers between devices: none -> 17.5 us  [exchange_in_pairs(): part = lax.ppermute(part, axis, [(d, d ^ mask) for d in range(ways)])]
    all_to_all x1 -> x0, blocking collectives: 13.7 us -> none  [shards(): lax.all_to_all(row_delta, 'head', split_axis=1, concat_axis=0, tiled=True)]
    all_to_all x1, waiting for transfers between devices: 6.59 us -> 0.8 us  [shards(): lax.all_to_all(value_heads, 'head', split_axis=1, concat_axis=0, tiled=True)]
    all_to_all x1, waiting for transfers between devices: 6.08 us -> 2.52 us  [shards(): lax.all_to_all(grad_heads, 'head', split_axis=1, concat_axis=0, tiled=True)]
    all_to_all x1, waiting for transfers between devices: 7.25 us -> 5.13 us  [shards(): lax.all_to_all(row_delta, 'head', split_axis=1, concat_axis=0, tiled=True)]
    unnamed x14 -> x16, local copies, waits for them, and re-layouts: 1.42 us -> 2.43 us
  transfers between devices with their start and end apart: 16 -> 23, of which waited for: 12 -> 12; matrix products, arithmetic and copies ran while one was open for 5% -> 7% of each run, Pallas kernels for 0% -> 0%
where the time goes in v1:
time: 109 us; the launch traced here: 108 us
  starting transfers between devices  47.3 us (43%)
  waiting for transfers between devices  45.2 us (41%)
  local copies, waits for them, and re-layouts  9.99 us (9%)
  matrix products  3.54 us (3%)
  other arithmetic  1.31 us (1%)
    ppermute x7, starting transfers between devices, exchange_in_pairs(): part = lax.ppermute(part, axis, [(d, d ^ mask) for d in range(ways)])  17.5 us
    all_to_all x1, waiting for transfers between devices, shards(): lax.all_to_all(key_grad, 'head', split_axis=0, concat_axis=1, tiled=True)  7.38 us
    all_to_all x1, waiting for transfers between devices, shards(): lax.all_to_all(value_grad, 'head', split_axis=0, concat_axis=1, tiled=True)  7.36 us
    all_to_all x1, waiting for transfers between devices, shards(): lax.all_to_all(query_heads, 'head', split_axis=1, concat_axis=0, tiled=True)  7.16 us
    all_to_all x1, waiting for transfers between devices, shards(): lax.all_to_all(query_grad.astype(jnp.bfloat16), 'head', split_axis=0, con...  6.6 us
    all_to_all x1, waiting for transfers between devices, shards(): lax.all_to_all(log_norm, 'head', split_axis=1, concat_axis=0, tiled=True)  6.43 us
    all_to_all x1, waiting for transfers between devices, shards(): lax.all_to_all(row_delta, 'head', split_axis=1, concat_axis=0, tiled=True)  5.13 us
    all_to_all x1, starting transfers between devices, shards(): lax.all_to_all(row_delta, 'head', split_axis=1, concat_axis=0, tiled=True)  3.78 us
  transfers between devices with their start and end apart: 23, of which 12 were waited for; matrix products, arithmetic and copies ran while one was open for 7% of the time, Pallas kernels for 0%

profile of v1, /device:TPU:0, one launch (start us, length us, event | category | flops | bytes accessed | tf_op | source)
XLA Modules:
  0.0 108.4 jit_solution(9648446895330462067)
XLA Ops:
  1.5 3.0 %collective-permute-start.4 = (bf16[32,2,128]{2,0,1:T(8,128)(2,1)S(1)}, bf16[32,2,128]{2,0,1:T(8,128)(2,1)S(1)}, u32[]{:S(2)}, u32[]{:S(2)}) collective-permute-start(bf16[32,2,128]{2,0,1:T(8,128)(2,1)S(1)} %get-tuple-element.679), channel_id=1, source_target_pairs={{0,2},{2,0},{4,6},{6,4},{8,10},{10,8},{12,14},{14,12},{1,3},{3,1},... | collective-permute-start | bytes 49160 | tf_op jit(solution)/shard_map/ppermute | solution.py:22
  4.5 1.6 %collective-permute-start.5 = (bf16[32,2,128]{2,0,1:T(8,128)(2,1)S(1)}, bf16[32,2,128]{2,0,1:T(8,128)(2,1)S(1)}, u32[]{:S(2)}, u32[]{:S(2)}) collective-permute-start(bf16[32,2,128]{2,0,1:T(8,128)(2,1)S(1)} %get-tuple-element.678), channel_id=1, source_target_pairs={{0,4},{2,6},{4,0},{6,2},{8,12},{10,14},{12,8},{14,10},{1,5},{3,7},... | collective-permute-start | bytes 49160 | tf_op jit(solution)/shard_map/ppermute | solution.py:22
  6.1 3.0 %collective-permute-start.7 = (bf16[32,2,128]{2,0,1:T(8,128)(2,1)S(1)}, bf16[32,2,128]{2,0,1:T(8,128)(2,1)S(1)}, u32[]{:S(2)}, u32[]{:S(2)}) collective-permute-start(bf16[32,2,128]{2,0,1:T(8,128)(2,1)S(1)} %get-tuple-element.676), channel_id=1, source_target_pairs={{0,8},{2,10},{4,12},{6,14},{8,0},{10,2},{12,4},{14,6},{1,9},{3,11}... | collective-permute-start | bytes 49160 | tf_op jit(solution)/shard_map/ppermute | solution.py:22
  10.9 3.8 %all-to-all-start.4 = ((f32[32,8,2]{0,2,1:T(2,128)}), f32[32,8,2]{0,2,1:T(2,128)S(1)}, u32[]{:S(2)}, u32[]{:S(2)}) async-start(f32[32,8,2]{0,2,1:T(2,128)} %bitcast.15), calls=%async_computation.4 | async-start | bytes 16384 | tf_op jit(solution)/shard_map/all_to_all | solution.py:104
  16.1 5.1 %all-to-all-done.4 = f32[32,8,2]{0,2,1:T(2,128)S(1)} async-done(((f32[32,8,2]{0,2,1:T(2,128)}), f32[32,8,2]{0,2,1:T(2,128)S(1)}, u32[]{:S(2)}, u32[]{:S(2)}) %all-to-all-start.4) | async-done | bytes 2080 | tf_op jit(solution)/shard_map/all_to_all | solution.py:104
  21.2 3.3 %all-to-all-start.2 = ((f32[32,8,2]{0,2,1:T(2,128)}), f32[32,8,2]{0,2,1:T(2,128)S(1)}, u32[]{:S(2)}, u32[]{:S(2)}) async-start(f32[32,8,2]{0,2,1:T(2,128)} %bitcast.10), calls=%async_computation.2 | async-start | bytes 16384 | tf_op jit(solution)/shard_map/all_to_all | solution.py:103
  24.5 6.4 %all-to-all-done.2 = f32[32,8,2]{0,2,1:T(2,128)S(1)} async-done(((f32[32,8,2]{0,2,1:T(2,128)}), f32[32,8,2]{0,2,1:T(2,128)S(1)}, u32[]{:S(2)}, u32[]{:S(2)}) %all-to-all-start.2) | async-done | bytes 2080 | tf_op jit(solution)/shard_map/all_to_all | solution.py:103
  31.7 3.5 %all-to-all-start = ((bf16[32,16,128]{2,0,1:T(8,128)(2,1)}), bf16[32,16,128]{2,0,1:T(8,128)(2,1)S(1)}, u32[]{:S(2)}, u32[]{:S(2)}) async-start(bf16[32,16,128]{2,0,1:T(8,128)(2,1)} %bitcast.1), calls=%async_computation | async-start | bytes 262144 | tf_op jit(solution)/shard_map/all_to_all | solution.py:100
  36.5 3.7 %collective-permute-start.8 = (bf16[32,2,128]{2,0,1:T(8,128)(2,1)S(1)}, bf16[32,2,128]{2,0,1:T(8,128)(2,1)S(1)}, u32[]{:S(2)}, u32[]{:S(2)}) collective-permute-start(bf16[32,2,128]{2,0,1:T(8,128)(2,1)S(1)} %get-tuple-element.675), channel_id=1, source_target_pairs={{0,10},{2,8},{4,14},{6,12},{8,2},{10,0},{12,6},{14,4},{1,11},{3,9}... | collective-permute-start | bytes 49160 | tf_op jit(solution)/shard_map/ppermute | solution.py:22
  40.2 1.4 %collective-permute-start.9 = (bf16[32,2,128]{2,0,1:T(8,128)(2,1)S(1)}, bf16[32,2,128]{2,0,1:T(8,128)(2,1)S(1)}, u32[]{:S(2)}, u32[]{:S(2)}) collective-permute-start(bf16[32,2,128]{2,0,1:T(8,128)(2,1)S(1)} %get-tuple-element.674), channel_id=1, source_target_pairs={{0,12},{2,14},{4,8},{6,10},{8,4},{10,6},{12,0},{14,2},{1,13},{3,15... | collective-permute-start | bytes 49160 | tf_op jit(solution)/shard_map/ppermute | solution.py:22
  42.5 3.4 %all-to-all-start.3 = ((bf16[32,16,128]{2,0,1:T(8,128)(2,1)}), bf16[32,16,128]{2,0,1:T(8,128)(2,1)S(1)}, u32[]{:S(2)}, u32[]{:S(2)}) async-start(bf16[32,16,128]{2,0,1:T(8,128)(2,1)} %copy_bitcast_fusion), calls=%async_computation.3 | async-start | bytes 262144 | tf_op jit(solution)/shard_map/all_to_all | solution.py:98
  45.9 4.7 %collective-permute-start.10 = (bf16[32,2,128]{2,0,1:T(8,128)(2,1)S(1)}, bf16[32,2,128]{2,0,1:T(8,128)(2,1)S(1)}, u32[]{:S(2)}, u32[]{:S(2)}) collective-permute-start(bf16[32,2,128]{2,0,1:T(8,128)(2,1)S(1)} %get-tuple-element.673), channel_id=1, source_target_pairs={{0,14},{2,12},{4,10},{6,8},{8,6},{10,4},{12,2},{14,0},{1,15},{3,13... | collective-permute-start | bytes 49160 | tf_op jit(solution)/shard_map/ppermute | solution.py:22
  50.6 2.5 %all-to-all-done.3 = bf16[32,16,128]{2,0,1:T(8,128)(2,1)S(1)} async-done(((bf16[32,16,128]{2,0,1:T(8,128)(2,1)}), bf16[32,16,128]{2,0,1:T(8,128)(2,1)S(1)}, u32[]{:S(2)}, u32[]{:S(2)}) %all-to-all-start.3) | async-done | bytes 131104 | tf_op jit(solution)/shard_map/all_to_all | solution.py:98
  53.1 3.4 %all-to-all-start.1 = ((bf16[32,16,128]{2,0,1:T(8,128)(2,1)}), bf16[32,16,128]{2,0,1:T(8,128)(2,1)S(1)}, u32[]{:S(2)}, u32[]{:S(2)}) async-start(bf16[32,16,128]{2,0,1:T(8,128)(2,1)} %copy_bitcast_fusion.1), calls=%async_computation.1 | async-start | bytes 262144 | tf_op jit(solution)/shard_map/all_to_all | solution.py:97
  56.6 7.2 %all-to-all-done.1 = bf16[32,16,128]{2,0,1:T(8,128)(2,1)S(1)} async-done(((bf16[32,16,128]{2,0,1:T(8,128)(2,1)}), bf16[32,16,128]{2,0,1:T(8,128)(2,1)S(1)}, u32[]{:S(2)}, u32[]{:S(2)}) %all-to-all-start.1) | async-done | bytes 131104 | tf_op jit(solution)/shard_map/all_to_all | solution.py:97
  63.8 8.2 %while.29 = (s32[]{:T(128)}, bf16[256,2,128]{2,0,1:T(8,128)(2,1)S(1)}, bf16[256,2,128]{2,0,1:T(8,128)(2,1)S(1)}, f32[256,2,128]{2,0,1:T(8,128)S(1)}, f32[256,2,1...) while((s32[]{:T(128)}, ...), condition=%wide.region_5.6_spmd.clone.clone.clone, body=%wide.region_2.5_spmd.clone.clone.clone.sunk | while | flops 172717072 | bytes 8807412 | solution.py:129
  73.0 3.4 %all-to-all-start.5 = ((bf16[256,2,128]{2,1,0:T(2,128)(2,1)}), bf16[256,2,128]{2,1,0:T(2,128)(2,1)S(1)}, u32[]{:S(2)}, u32[]{:S(2)}) async-start(bf16[256,2,128]{2,1,0:T(2,128)(2,1)} %copy.123), calls=%async_computation.5 | async-start | bytes 262144 | tf_op jit(solution)/shard_map/all_to_all | solution.py:131
  76.3 0.9 copy.102
  77.2 6.6 %all-to-all-done.5 = bf16[256,2,128]{2,1,0:T(2,128)(2,1)S(1)} async-done(((bf16[256,2,128]{2,1,0:T(2,128)(2,1)}), bf16[256,2,128]{2,1,0:T(2,128)(2,1)S(1)}, u32[]{:S(2)}, u32[]{:S(2)}) %all-to-all-start.5) | async-done | bytes 131104 | tf_op jit(solution)/shard_map/all_to_all | solution.py:131
  83.8 3.4 %all-to-all-start.6 = ((f32[256,2,128]{2,1,0:T(2,128)}), f32[256,2,128]{2,1,0:T(2,128)S(1)}, u32[]{:S(2)}, u32[]{:S(2)}) async-start(f32[256,2,128]{2,1,0:T(2,128)} %copy.102), calls=%async_computation.6 | async-start | bytes 524288 | tf_op jit(solution)/shard_map/all_to_all | solution.py:136
  87.3 0.9 copy.104
  88.2 7.4 %all-to-all-done.6 = f32[256,2,128]{2,1,0:T(2,128)S(1)} async-done(((f32[256,2,128]{2,1,0:T(2,128)}), f32[256,2,128]{2,1,0:T(2,128)S(1)}, u32[]{:S(2)}, u32[]{:S(2)}) %all-to-all-start.6) | async-done | bytes 262176 | tf_op jit(solution)/shard_map/all_to_all | solution.py:136
  95.5 3.4 %all-to-all-start.7 = ((f32[256,2,128]{2,1,0:T(2,128)}), f32[256,2,128]{2,1,0:T(2,128)S(1)}, u32[]{:S(2)}, u32[]{:S(2)}) async-start(f32[256,2,128]{2,1,0:T(2,128)} %copy.104), calls=%async_computation.7 | async-start | bytes 524288 | tf_op jit(solution)/shard_map/all_to_all | solution.py:137
  100.1 7.4 %all-to-all-done.7 = f32[256,2,128]{2,1,0:T(2,128)S(1)} async-done(((f32[256,2,128]{2,1,0:T(2,128)}), f32[256,2,128]{2,1,0:T(2,128)S(1)}, u32[]{:S(2)}, u32[]{:S(2)}) %all-to-all-start.7) | async-done | bytes 262176 | tf_op jit(solution)/shard_map/all_to_all | solution.py:137
  (108 shorter events, 17.9 us)
Async XLA Ops:
  0.6 14.7 %copy-start = (bf16[32,2048]{1,0:T(8,128)(2,1)S(1)}, bf16[32,2048]{1,0:T(8,128)(2,1)}, u32[]{:S(2)}) copy-start(bf16[32,2048]{1,0:T(8,128)(2,1)} %param.10) | copy-start | bytes 393220
  1.5 38.7 %collective-permute-start.4 = (bf16[32,2,128]{2,0,1:T(8,128)(2,1)S(1)}, bf16[32,2,128]{2,0,1:T(8,128)(2,1)S(1)}, u32[]{:S(2)}, u32[]{:S(2)}) collective-permute-start(bf16[32,2,128]{2,0,1:T(8,128)(2,1)S(1)} %get-tuple-element.679), channel_id=1, source_target_pairs={{0,2},{2,0},{4,6},{6,4},{8,10},{10,8},{12,14},{14,12},{1,3},{3,1},... | collective-permute-start | bytes 49160 | tf_op jit(solution)/shard_map/ppermute | solution.py:22
  4.5 41.3 %collective-permute-start.5 = (bf16[32,2,128]{2,0,1:T(8,128)(2,1)S(1)}, bf16[32,2,128]{2,0,1:T(8,128)(2,1)S(1)}, u32[]{:S(2)}, u32[]{:S(2)}) collective-permute-start(bf16[32,2,128]{2,0,1:T(8,128)(2,1)S(1)} %get-tuple-element.678), channel_id=1, source_target_pairs={{0,4},{2,6},{4,0},{6,2},{8,12},{10,14},{12,8},{14,10},{1,5},{3,7},... | collective-permute-start | bytes 49160 | tf_op jit(solution)/shard_map/ppermute | solution.py:22
  6.1 44.5 %collective-permute-start.6 = (bf16[32,2,128]{2,0,1:T(8,128)(2,1)S(1)}, bf16[32,2,128]{2,0,1:T(8,128)(2,1)S(1)}, u32[]{:S(2)}, u32[]{:S(2)}) collective-permute-start(bf16[32,2,128]{2,0,1:T(8,128)(2,1)S(1)} %get-tuple-element.677), channel_id=1, source_target_pairs={{0,6},{2,4},{4,2},{6,0},{8,14},{10,12},{12,10},{14,8},{1,7},{3,5},... | collective-permute-start | bytes 49160 | tf_op jit(solution)/shard_map/ppermute | solution.py:22
  6.1 44.5 %collective-permute-start.7 = (bf16[32,2,128]{2,0,1:T(8,128)(2,1)S(1)}, bf16[32,2,128]{2,0,1:T(8,128)(2,1)S(1)}, u32[]{:S(2)}, u32[]{:S(2)}) collective-permute-start(bf16[32,2,128]{2,0,1:T(8,128)(2,1)S(1)} %get-tuple-element.676), channel_id=1, source_target_pairs={{0,8},{2,10},{4,12},{6,14},{8,0},{10,2},{12,4},{14,6},{1,9},{3,11}... | collective-permute-start | bytes 49160 | tf_op jit(solution)/shard_map/ppermute | solution.py:22
  10.9 10.3 %all-to-all-start.4 = ((f32[32,8,2]{0,2,1:T(2,128)}), f32[32,8,2]{0,2,1:T(2,128)S(1)}, u32[]{:S(2)}, u32[]{:S(2)}) async-start(f32[32,8,2]{0,2,1:T(2,128)} %bitcast.15), calls=%async_computation.4 | async-start | bytes 16384 | tf_op jit(solution)/shard_map/all_to_all | solution.py:104
  21.2 9.8 %all-to-all-start.2 = ((f32[32,8,2]{0,2,1:T(2,128)}), f32[32,8,2]{0,2,1:T(2,128)S(1)}, u32[]{:S(2)}, u32[]{:S(2)}) async-start(f32[32,8,2]{0,2,1:T(2,128)} %bitcast.10), calls=%async_computation.2 | async-start | bytes 16384 | tf_op jit(solution)/shard_map/all_to_all | solution.py:103
  31.7 10.8 %all-to-all-start = ((bf16[32,16,128]{2,0,1:T(8,128)(2,1)}), bf16[32,16,128]{2,0,1:T(8,128)(2,1)S(1)}, u32[]{:S(2)}, u32[]{:S(2)}) async-start(bf16[32,16,128]{2,0,1:T(8,128)(2,1)} %bitcast.1), calls=%async_computation | async-start | bytes 262144 | tf_op jit(solution)/shard_map/all_to_all | solution.py:100
  36.5 20.0 %collective-permute-start.8 = (bf16[32,2,128]{2,0,1:T(8,128)(2,1)S(1)}, bf16[32,2,128]{2,0,1:T(8,128)(2,1)S(1)}, u32[]{:S(2)}, u32[]{:S(2)}) collective-permute-start(bf16[32,2,128]{2,0,1:T(8,128)(2,1)S(1)} %get-tuple-element.675), channel_id=1, source_target_pairs={{0,10},{2,8},{4,14},{6,12},{8,2},{10,0},{12,6},{14,4},{1,11},{3,9}... | collective-permute-start | bytes 49160 | tf_op jit(solution)/shard_map/ppermute | solution.py:22
  40.2 16.3 %collective-permute-start.9 = (bf16[32,2,128]{2,0,1:T(8,128)(2,1)S(1)}, bf16[32,2,128]{2,0,1:T(8,128)(2,1)S(1)}, u32[]{:S(2)}, u32[]{:S(2)}) collective-permute-start(bf16[32,2,128]{2,0,1:T(8,128)(2,1)S(1)} %get-tuple-element.674), channel_id=1, source_target_pairs={{0,12},{2,14},{4,8},{6,10},{8,4},{10,6},{12,0},{14,2},{1,13},{3,15... | collective-permute-start | bytes 49160 | tf_op jit(solution)/shard_map/ppermute | solution.py:22
  42.5 10.7 %all-to-all-start.3 = ((bf16[32,16,128]{2,0,1:T(8,128)(2,1)}), bf16[32,16,128]{2,0,1:T(8,128)(2,1)S(1)}, u32[]{:S(2)}, u32[]{:S(2)}) async-start(bf16[32,16,128]{2,0,1:T(8,128)(2,1)} %copy_bitcast_fusion), calls=%async_computation.3 | async-start | bytes 262144 | tf_op jit(solution)/shard_map/all_to_all | solution.py:98
  45.9 10.7 %collective-permute-start.10 = (bf16[32,2,128]{2,0,1:T(8,128)(2,1)S(1)}, bf16[32,2,128]{2,0,1:T(8,128)(2,1)S(1)}, u32[]{:S(2)}, u32[]{:S(2)}) collective-permute-start(bf16[32,2,128]{2,0,1:T(8,128)(2,1)S(1)} %get-tuple-element.673), channel_id=1, source_target_pairs={{0,14},{2,12},{4,10},{6,8},{8,6},{10,4},{12,2},{14,0},{1,15},{3,13... | collective-permute-start | bytes 49160 | tf_op jit(solution)/shard_map/ppermute | solution.py:22
  53.1 10.7 %all-to-all-start.1 = ((bf16[32,16,128]{2,0,1:T(8,128)(2,1)}), bf16[32,16,128]{2,0,1:T(8,128)(2,1)S(1)}, u32[]{:S(2)}, u32[]{:S(2)}) async-start(bf16[32,16,128]{2,0,1:T(8,128)(2,1)} %copy_bitcast_fusion.1), calls=%async_computation.1 | async-start | bytes 262144 | tf_op jit(solution)/shard_map/all_to_all | solution.py:97
  65.4 2.5 %collective-permute-start.2 = (f32[256,2,128]{2,0,1:T(8,128)S(1)}, f32[256,2,128]{2,0,1:T(8,128)S(1)}, u32[]{:S(2)}, u32[]{:S(2)}) collective-permute-start(f32[256,2,128]{2,0,1:T(8,128)S(1)} %fusion.84), channel_id=1, source_target_pairs={{0,1},{1,0},{2,3},{3,2},{4,5},{5,4},{6,7},{7,6},{8,9},{9,8},{10,11... | collective-permute-start | bytes 786440 | tf_op jit(solution)/shard_map/while/body/eval_jaxpr/ppermute | solution.py:30
  65.8 2.1 %collective-permute-start.3 = (f32[256,2,128]{2,0,1:T(8,128)S(1)}, f32[256,2,128]{2,0,1:T(8,128)S(1)}, u32[]{:S(2)}, u32[]{:S(2)}) collective-permute-start(f32[256,2,128]{2,0,1:T(8,128)S(1)} %fusion.85), channel_id=1, source_target_pairs={{0,1},{1,0},{2,3},{3,2},{4,5},{5,4},{6,7},{7,6},{8,9},{9,8},{10,11... | collective-permute-start | bytes 786440 | tf_op jit(solution)/shard_map/while/body/eval_jaxpr/ppermute | solution.py:30
  66.3 1.3 %collective-permute-start = (bf16[256,2,128]{2,0,1:T(8,128)(2,1)S(1)}, bf16[256,2,128]{2,0,1:T(8,128)(2,1)S(1)}, u32[]{:S(2)}, u32[]{:S(2)}) collective-permute-start(bf16[256,2,128]{2,0,1:T(8,128)(2,1)S(1)} %copy.141), channel_id=1, source_target_pairs={{0,1},{1,0},{2,3},{3,2},{4,5},{5,4},{6,7},{7,6},{8,9},{9,8},{10,11... | collective-permute-start | bytes 393224 | tf_op jit(solution)/shard_map/while/body/eval_jaxpr/ppermute | solution.py:30
  66.4 1.5 %collective-permute-start.1 = (bf16[256,2,128]{2,0,1:T(8,128)(2,1)S(1)}, bf16[256,2,128]{2,0,1:T(8,128)(2,1)S(1)}, u32[]{:S(2)}, u32[]{:S(2)}) collective-permute-start(bf16[256,2,128]{2,0,1:T(8,128)(2,1)S(1)} %copy.142), channel_id=1, source_target_pairs={{0,1},{1,0},{2,3},{3,2},{4,5},{5,4},{6,7},{7,6},{8,9},{9,8},{10,11... | collective-permute-start | bytes 393224 | tf_op jit(solution)/shard_map/while/body/eval_jaxpr/ppermute | solution.py:30
  69.4 2.7 %collective-permute-start.2 = (f32[256,2,128]{2,0,1:T(8,128)S(1)}, f32[256,2,128]{2,0,1:T(8,128)S(1)}, u32[]{:S(2)}, u32[]{:S(2)}) collective-permute-start(f32[256,2,128]{2,0,1:T(8,128)S(1)} %fusion.84), channel_id=1, source_target_pairs={{0,1},{1,0},{2,3},{3,2},{4,5},{5,4},{6,7},{7,6},{8,9},{9,8},{10,11... | collective-permute-start | bytes 786440 | tf_op jit(solution)/shard_map/while/body/eval_jaxpr/ppermute | solution.py:30
  70.1 2.0 %collective-permute-start.3 = (f32[256,2,128]{2,0,1:T(8,128)S(1)}, f32[256,2,128]{2,0,1:T(8,128)S(1)}, u32[]{:S(2)}, u32[]{:S(2)}) collective-permute-start(f32[256,2,128]{2,0,1:T(8,128)S(1)} %fusion.85), channel_id=1, source_target_pairs={{0,1},{1,0},{2,3},{3,2},{4,5},{5,4},{6,7},{7,6},{8,9},{9,8},{10,11... | collective-permute-start | bytes 786440 | tf_op jit(solution)/shard_map/while/body/eval_jaxpr/ppermute | solution.py:30
  70.3 1.6 %collective-permute-start = (bf16[256,2,128]{2,0,1:T(8,128)(2,1)S(1)}, bf16[256,2,128]{2,0,1:T(8,128)(2,1)S(1)}, u32[]{:S(2)}, u32[]{:S(2)}) collective-permute-start(bf16[256,2,128]{2,0,1:T(8,128)(2,1)S(1)} %copy.141), channel_id=1, source_target_pairs={{0,1},{1,0},{2,3},{3,2},{4,5},{5,4},{6,7},{7,6},{8,9},{9,8},{10,11... | collective-permute-start | bytes 393224 | tf_op jit(solution)/shard_map/while/body/eval_jaxpr/ppermute | solution.py:30
  70.7 1.4 %collective-permute-start.1 = (bf16[256,2,128]{2,0,1:T(8,128)(2,1)S(1)}, bf16[256,2,128]{2,0,1:T(8,128)(2,1)S(1)}, u32[]{:S(2)}, u32[]{:S(2)}) collective-permute-start(bf16[256,2,128]{2,0,1:T(8,128)(2,1)S(1)} %copy.142), channel_id=1, source_target_pairs={{0,1},{1,0},{2,3},{3,2},{4,5},{5,4},{6,7},{7,6},{8,9},{9,8},{10,11... | collective-permute-start | bytes 393224 | tf_op jit(solution)/shard_map/while/body/eval_jaxpr/ppermute | solution.py:30
  73.0 10.9 %all-to-all-start.5 = ((bf16[256,2,128]{2,1,0:T(2,128)(2,1)}), bf16[256,2,128]{2,1,0:T(2,128)(2,1)S(1)}, u32[]{:S(2)}, u32[]{:S(2)}) async-start(bf16[256,2,128]{2,1,0:T(2,128)(2,1)} %copy.123), calls=%async_computation.5 | async-start | bytes 262144 | tf_op jit(solution)/shard_map/all_to_all | solution.py:131
  83.8 11.7 %all-to-all-start.6 = ((f32[256,2,128]{2,1,0:T(2,128)}), f32[256,2,128]{2,1,0:T(2,128)S(1)}, u32[]{:S(2)}, u32[]{:S(2)}) async-start(f32[256,2,128]{2,1,0:T(2,128)} %copy.102), calls=%async_computation.6 | async-start | bytes 524288 | tf_op jit(solution)/shard_map/all_to_all | solution.py:136
  95.5 11.9 %all-to-all-start.7 = ((f32[256,2,128]{2,1,0:T(2,128)}), f32[256,2,128]{2,1,0:T(2,128)S(1)}, u32[]{:S(2)}, u32[]{:S(2)}) async-start(f32[256,2,128]{2,1,0:T(2,128)} %copy.104), calls=%async_computation.7 | async-start | bytes 524288 | tf_op jit(solution)/shard_map/all_to_all | solution.py:137
  (6 other events, 14.3 us)
